TPU v7x, 256 devices: a whole 4x4x8 slice. The times are simulated.
256 devices in a mesh: sy: 16 (over x, y_hi, core), sx: 16 (over y_lo, z).
Axes of the slice: x: 4, y: 4 (y_hi: 2, y_lo: 2; y = y_hi * 2 + y_lo), z: 8, core: 2. Of those that a mesh axis runs over, the one named last changes fastest.
Arguments:
- object_tile: float32 [2, 2048, 2048], P(None, 'sy', 'sx'), may hold values from -5 to 5
- probe_modes: float32 [2, 2, 128, 128], replicated, may hold values from -4 to 4
- scan_offsets: int32 [16, 16, 4, 2], P('sy', 'sx'), may hold values from 0 to 128
- intensities: float32 [16, 16, 4, 128, 128], P('sy', 'sx'), may hold values from 0 to 2
Outputs:
- object_out: float32 [2, 2048, 2048], P(None, 'sy', 'sx')
- probe_out: float32 [2, 2, 128, 128], replicated
Inputs may be any that keep to these rules, and one draw needn't show every extreme that they name: `scan_offsets`: offsets are counted from 64 pixels above and to the left of the device's tile, so a patch stays within 64 pixels of its tile.
All inputs are finite; a program needn't handle non-finite values.
Results may differ from a plain program's by a relative error of at most 0.0003.
Values sent between devices are 32-bit elements; how exact they have to be, the bound alone decides.
A program may use at most 64 MiB of HBM per device.

v0:
```python
import jax
import jax.numpy as jnp
from jax import lax
from jax.sharding import PartitionSpec as P

ITERS = 2
HIGHEST = lax.Precision.HIGHEST
OBJECT_STEP = 0.5
PROBE_STEP = 2.0
REGULAR = 1.0


def extended(block, sides, width):
    for axis, dim in sides:
        count = lax.axis_size(axis)
        forward = [(i, i + 1) for i in range(count - 1)]
        backward = [(target, source) for source, target in forward]
        low = lax.ppermute(
            lax.slice_in_dim(block, block.shape[dim] - width, None, axis=dim), axis, forward
        )
        high = lax.ppermute(lax.slice_in_dim(block, 0, width, axis=dim), axis, backward)
        block = jnp.concatenate([low, block, high], axis=dim)
    return block


def shifted(value, axis, steps):
    count = lax.axis_size(axis)
    first, last = (max(0, -steps), min(count, count - steps))
    return lax.ppermute(value, axis, [(source, source + steps) for source in range(first, last)])


def tables(extent):
    index_line = jnp.arange(extent, dtype=jnp.int32)
    phase = index_line[:, None] * index_line[None, :] % extent
    angle = phase.astype(jnp.float32) * (2.0 * jnp.pi / extent)
    scale = 1.0 / jnp.sqrt(jnp.float32(extent))
    return (jnp.cos(angle) * scale, jnp.sin(angle) * scale)


def apply_left(matrix, values):
    return jnp.einsum("ux,bxy->buy", matrix, values, precision=HIGHEST)


def apply_right(values, matrix):
    return jnp.einsum("bxy,yv->bxv", values, matrix, precision=HIGHEST)


def transform(real_part, imag_part, cosine_table, sine_table, direction):
    half_real = apply_left(cosine_table, real_part) + direction * apply_left(sine_table, imag_part)
    half_imag = apply_left(cosine_table, imag_part) - direction * apply_left(sine_table, real_part)
    out_real = apply_right(half_real, cosine_table) + direction * apply_right(half_imag, sine_table)
    out_imag = apply_right(half_imag, cosine_table) - direction * apply_right(half_real, sine_table)
    return (out_real, out_imag)


def local_terms(canvas, probe_modes, offsets, measured):
    extent = probe_modes.shape[-1]
    mode_count = probe_modes.shape[0]
    positions = offsets.shape[0]
    patches = jax.vmap(
        lambda corner: lax.dynamic_slice(
            canvas, (jnp.int32(0), corner[0], corner[1]), (2, extent, extent)
        )
    )(offsets)
    object_real = patches[:, 0][:, None]
    object_imag = patches[:, 1][:, None]
    probe_real = probe_modes[:, 0][None]
    probe_imag = probe_modes[:, 1][None]
    exit_real = (probe_real * object_real - probe_imag * object_imag).reshape(
        positions * mode_count, extent, extent
    )
    exit_imag = (probe_real * object_imag + probe_imag * object_real).reshape(
        positions * mode_count, extent, extent
    )
    cosine_table, sine_table = tables(extent)
    spectrum_real, spectrum_imag = transform(exit_real, exit_imag, cosine_table, sine_table, 1.0)
    spectrum_real = spectrum_real.reshape(positions, mode_count, extent, extent)
    spectrum_imag = spectrum_imag.reshape(positions, mode_count, extent, extent)
    misfit = (
        jnp.sum(spectrum_real * spectrum_real + spectrum_imag * spectrum_imag, axis=1) - measured
    )
    back_real, back_imag = transform(
        (misfit[:, None] * spectrum_real).reshape(-1, extent, extent),
        (misfit[:, None] * spectrum_imag).reshape(-1, extent, extent),
        cosine_table,
        sine_table,
        -1.0,
    )
    back_real = back_real.reshape(positions, mode_count, extent, extent)
    back_imag = back_imag.reshape(positions, mode_count, extent, extent)
    grad_real = jnp.sum(probe_real * back_real + probe_imag * back_imag, axis=1)
    grad_imag = jnp.sum(probe_real * back_imag - probe_imag * back_real, axis=1)
    lighting = jnp.broadcast_to(
        jnp.sum(probe_real * probe_real + probe_imag * probe_imag, axis=1), grad_real.shape
    )
    terms = jnp.stack([grad_real, grad_imag, lighting], axis=1)
    numer_real = jnp.sum(object_real * back_real + object_imag * back_imag, axis=0)
    numer_imag = jnp.sum(object_real * back_imag - object_imag * back_real, axis=0)
    numerator = jnp.stack([numer_real, numer_imag], axis=1)
    denominator = jnp.sum(
        object_real[:, 0] * object_real[:, 0] + object_imag[:, 0] * object_imag[:, 0], axis=0
    )

    def place_patch(number, running):
        corner = offsets[number]
        existing = lax.dynamic_slice(
            running, (jnp.int32(0), corner[0], corner[1]), (3, extent, extent)
        )
        return lax.dynamic_update_slice(
            running, existing + terms[number], (jnp.int32(0), corner[0], corner[1])
        )

    gradients = lax.fori_loop(
        0, positions, place_patch, jnp.zeros((3,) + canvas.shape[1:], jnp.float32)
    )
    return (gradients, numerator, denominator)


def probe_update(probe_modes, numerator, denominator):
    extent = probe_modes.shape[-1]
    flat_numer = numerator.reshape(-1, extent * extent)
    flat_denom = denominator.reshape(extent * extent)
    flat_probe = probe_modes.reshape(-1, extent * extent)
    total_numer, total_denom = lax.psum((flat_numer, flat_denom), ("sy", "sx"))
    updated = flat_probe - PROBE_STEP * total_numer / (total_denom[None] + REGULAR)
    return updated.reshape(probe_modes.shape)


def fetch(current, halo_width):
    return extended(current, (("sy", 1), ("sx", 2)), halo_width)


def owner_sum(gradients, tile_size, halo_width):
    upper_rim = gradients[:, :halo_width]
    lower_rim = gradients[:, halo_width + tile_size :]
    from_above = shifted(lower_rim, "sy", 1)
    from_below = shifted(upper_rim, "sy", -1)
    middle = gradients[:, halo_width : halo_width + tile_size]
    middle = (
        middle.at[:, :halo_width].add(from_above).at[:, tile_size - halo_width :].add(from_below)
    )
    left_rim = middle[:, :, :halo_width]
    right_rim = middle[:, :, halo_width + tile_size :]
    from_left = shifted(right_rim, "sx", 1)
    from_right = shifted(left_rim, "sx", -1)
    owned = middle[:, :, halo_width : halo_width + tile_size]
    return (
        owned.at[:, :, :halo_width]
        .add(from_left)
        .at[:, :, tile_size - halo_width :]
        .add(from_right)
    )


def per_device(object_tile, probe_modes, scan_offsets, intensities):
    tile_size = object_tile.shape[1]
    halo_width = probe_modes.shape[-1] // 2
    offsets = scan_offsets[0, 0]
    measured = intensities[0, 0]
    current = object_tile
    for iteration in range(ITERS):
        canvas = fetch(current, halo_width)
        gradients, numerator, denominator = local_terms(canvas, probe_modes, offsets, measured)
        owned = owner_sum(gradients, tile_size, halo_width)
        fresh_probe = probe_update(probe_modes, numerator, denominator)
        current = current - OBJECT_STEP * owned[:2] / (owned[2:3] + REGULAR)
        probe_modes = fresh_probe
    return (current, probe_modes)


def solution(mesh):
    placed = (P(None, "sy", "sx"), P(), P("sy", "sx", None, None), P("sy", "sx", None, None, None))
    return jax.shard_map(
        per_device,
        mesh=mesh,
        in_specs=placed,
        out_specs=(P(None, "sy", "sx"), P()),
        check_vma=False,
    )
```

profile of v0, /device:TPU:8, one launch (start us, length us, event | category | flops | bytes accessed | tf_op | source)
XLA Modules:
  0.0 710.8 jit_solution(12127745365018270601)
XLA Ops:
  8.1 1.9 collective-permute-start
  11.5 3.7 collective-permute-done.1
  15.4 3.8 collective-permute-start.2
  19.2 6.6 collective-permute-start.3
  25.9 2.4 collective-permute-done.2
  30.1 8.2 %while.38 = (s32[]{:T(128)}, f32[2,256,256]{2,1,0:T(8,128)S(1)}, s32[4,3]{1,0:T(4,128)S(1)}, f32[4,2,128,128]{3,2,1,0:T(8,128)S(1)}, s32[]{:T(128)}) while((s32[]{:T(128)}, f32[2,256,256]{2,1,0:T(8,128)S(1)}, s32[4,3]{1,0:T(4,128)S(1)}, f32[4,2,128,128]{3,2,1,0:T(8,128)S(1)}, s32[]{:T(128)}) %tuple.147), condition=%wide.while_cond.8, body=%wide.while_body.8.sunk | while | flops 2 | bytes 262261 | solution.py:61
  56.5 2.0 add_reduce_fusion.3
  58.7 29.5 %while.36 = (s32[]{:T(128)}, f32[3,256,256]{2,1,0:T(8,128)S(1)}, s32[4,2]{0,1:T(2,128)S(1)}, f32[4,3,128,128]{3,2,1,0:T(8,128)S(1)}, s32[]{:T(128)}, /*index=5*/s32[]{:T(128)}, s32[]{:T(128)}) while((s32[]{:T(128)}, f32[3,256,256]{2,1,0:T(8,128)S(1)}, s32[4,2]{0,1:T(2,128)S(1)}, f32[4,3,128,128]{3,2,1,0:T(8,128)S(1)}, s32[]{:T(128)}, ...), condition=%wide.region_5.6_spmd, body=%wide.region_4.5_spmd.sunk | while | flops 49160 | bytes 983237 | solution.py:113
  63.2 2.9 dynamic_update_slice.16
  70.7 2.8 dynamic_update_slice.16
  78.0 2.8 dynamic_update_slice.16
  85.4 2.8 dynamic_update_slice.16
  88.9 6.5 collective-permute-start.4
  100.6 1.9 collective-permute-start.6
  102.6 246.5 %all-reduce.7.cloned.1.call-done = (f32[4,16384]{1,0:T(4,128)}, f32[16384]{0:T(1024)}) async-done(((f32[4,16384]{1,0:T(4,128)}, f32[16384]{0:T(1024)}), (f32[4,16384]{1,0:T(4,128)}, f32[16384]{0:T(1024)})) %all-reduce.7.cloned.1.call-update) | async-done | bytes 327696 | tf_op jit(solution)/shard_map/psum | solution.py:124
  350.0 1.9 collective-permute-start.7
  352.6 6.3 collective-permute-done.7
  364.0 3.6 collective-permute-done.9
  367.8 2.5 collective-permute-start.10
  370.3 5.4 collective-permute-start.11
  375.8 2.4 collective-permute-done.10
  379.9 8.3 %while.39 = (s32[]{:T(128)}, f32[2,256,256]{2,1,0:T(8,128)S(1)}, s32[4,3]{1,0:T(4,128)S(1)}, f32[4,2,128,128]{3,2,1,0:T(8,128)S(1)}, s32[]{:T(128)}) while((s32[]{:T(128)}, f32[2,256,256]{2,1,0:T(8,128)S(1)}, s32[4,3]{1,0:T(4,128)S(1)}, f32[4,2,128,128]{3,2,1,0:T(8,128)S(1)}, s32[]{:T(128)}) %tuple.167), condition=%wide.while_cond.9, body=%wide.while_body.9.sunk | while | flops 2 | bytes 262261 | solution.py:61
  408.8 29.5 %while.37 = (s32[]{:T(128)}, f32[3,256,256]{2,1,0:T(8,128)S(1)}, s32[4,2]{0,1:T(2,128)S(1)}, f32[4,3,128,128]{3,2,1,0:T(8,128)S(1)}, s32[]{:T(128)}, /*index=5*/s32[]{:T(128)}, s32[]{:T(128)}) while((s32[]{:T(128)}, f32[3,256,256]{2,1,0:T(8,128)S(1)}, s32[4,2]{0,1:T(2,128)S(1)}, f32[4,3,128,128]{3,2,1,0:T(8,128)S(1)}, s32[]{:T(128)}, ...), condition=%wide.region_16.17_spmd, body=%wide.region_15.16_spmd.sunk | while | flops 49160 | bytes 983237 | solution.py:113
  413.4 2.9 dynamic_update_slice.17
  420.9 2.8 dynamic_update_slice.17
  428.2 2.8 dynamic_update_slice.17
  435.6 2.8 dynamic_update_slice.17
  438.5 5.4 collective-permute-start.12
  445.2 242.4 %all-reduce.5.cloned.1.call-done = (f32[4,16384]{1,0:T(4,128)}, f32[16384]{0:T(1024)}) async-done(((f32[4,16384]{1,0:T(4,128)}, f32[16384]{0:T(1024)}), (f32[4,16384]{1,0:T(4,128)}, f32[16384]{0:T(1024)})) %all-reduce.5.cloned.1.call-update) | async-done | bytes 327696 | tf_op jit(solution)/shard_map/psum | solution.py:124
  688.6 3.2 collective-permute-start.14
  692.8 4.7 collective-permute-start.15
  697.6 2.0 collective-permute-done.14
  (195 shorter events, 86.8 us)
Async XLA Ops:
  7.2 341.9 %all-reduce.7.cloned.1.call-start = ((), (), s32[]{:S(2)}) async-start(), calls=%async_computation.1 | async-start | bytes 655360 | tf_op jit(solution)/shard_map/psum | solution.py:124
  7.2 4.1 copy-start.11
  8.1 3.4 copy-start.3
  8.1 3.3 collective-permute-start
  10.0 5.2 collective-permute-start.1
  15.2 10.6 %copy-start.7 = (f32[2,2,128,128]{3,2,1,0:T(8,128)S(1)}, f32[2,2,128,128]{3,2,1,0:T(8,128)}, u32[]{:S(2)}) copy-start(f32[2,2,128,128]{3,2,1,0:T(8,128)} %param.25) | copy-start | bytes 786436
  15.4 12.9 %collective-permute-start.2 = (f32[2,256,64]{2,1,0:T(8,128)S(1)}, f32[2,256,64]{2,1,0:T(8,128)S(1)}, u32[]{:S(2)}, u32[]{:S(2)}) collective-permute-start(f32[2,256,64]{2,1,0:T(8,128)S(1)} %get-tuple-element.354), channel_id=1, source_target_pairs={{0,1},{1,2},{2,3},{3,4},{4,5},{5,6},{6,7},{7,8},{8,9},{9,10},{10,1... | collective-permute-start | bytes 393224 | tf_op jit(solution)/shard_map/ppermute | solution.py:18
  19.2 10.5 %collective-permute-start.3 = (f32[2,256,64]{2,1,0:T(8,128)S(1)}, f32[2,256,64]{2,1,0:T(8,128)S(1)}, u32[]{:S(2)}, u32[]{:S(2)}) collective-permute-start(f32[2,256,64]{2,1,0:T(8,128)S(1)} %get-tuple-element.355), channel_id=1, source_target_pairs={{1,0},{2,1},{3,2},{4,3},{5,4},{6,5},{7,6},{8,7},{9,8},{10,9},{11,1... | collective-permute-start | bytes 393224 | tf_op jit(solution)/shard_map/ppermute | solution.py:21
  38.3 0.7 copy-start
  46.9 1.2 copy-start.5
  88.9 7.8 %copy-start.1 = (f32[4,128,128]{2,1,0:T(8,128)S(1)}, f32[4,128,128]{2,1,0:T(8,128)}, u32[]{:S(2)}) copy-start(f32[4,128,128]{2,1,0:T(8,128)} %copy-done) | copy-start | bytes 786436
  88.9 7.8 %copy-start.2 = (f32[8,128,128]{2,1,0:T(8,128)S(1)}, f32[8,128,128]{2,1,0:T(8,128)}, u32[]{:S(2)}) copy-start(f32[8,128,128]{2,1,0:T(8,128)} %get-tuple-element.367) | copy-start | bytes 1572868
  88.9 9.6 %collective-permute-start.4 = (f32[3,64,256]{2,1,0:T(8,128)}, f32[3,64,256]{2,1,0:T(8,128)}, u32[]{:S(2)}, u32[]{:S(2)}) collective-permute-start(f32[3,64,256]{2,1,0:T(8,128)} %get-tuple-element.339), channel_id=1, source_target_pairs={{0,16},{16,32},{32,48},{48,64},{64,80},{80,96},{96,112},{112,128},... | collective-permute-start | bytes 589832 | tf_op jit(solution)/shard_map/ppermute | solution.py:29
  95.4 4.1 collective-permute-start.5
  98.5 589.0 %all-reduce.5.cloned.1.call-start = ((), (), s32[]{:S(2)}) async-start(), calls=%async_computation | async-start | bytes 655360 | tf_op jit(solution)/shard_map/psum | solution.py:124
  100.6 251.3 %collective-permute-start.6 = (f32[3,128,64]{2,1,0:T(8,128)S(1)}, f32[3,128,64]{2,1,0:T(8,128)S(1)}, u32[]{:S(2)}, u32[]{:S(2)}) collective-permute-start(f32[3,128,64]{2,1,0:T(8,128)S(1)} %get-tuple-element.345), channel_id=1, source_target_pairs={{0,1},{1,2},{2,3},{3,4},{4,5},{5,6},{6,7},{7,8},{8,9},{9,10},{10,1... | collective-permute-start | bytes 294920 | tf_op jit(solution)/shard_map/ppermute | solution.py:29
  350.0 8.8 %collective-permute-start.7 = (f32[3,128,64]{2,1,0:T(8,128)S(1)}, f32[3,128,64]{2,1,0:T(8,128)S(1)}, u32[]{:S(2)}, u32[]{:S(2)}) collective-permute-start(f32[3,128,64]{2,1,0:T(8,128)S(1)} %get-tuple-element.344), channel_id=1, source_target_pairs={{1,0},{2,1},{3,2},{4,3},{5,4},{6,5},{7,6},{8,7},{9,8},{10,9},{11,1... | collective-permute-start | bytes 294920 | tf_op jit(solution)/shard_map/ppermute | solution.py:29
  360.0 0.9 copy-start.4
  360.9 2.8 copy-start.8
  360.9 2.8 copy-start.9
  361.0 3.0 collective-permute-start.8
  362.4 5.2 collective-permute-start.9
  367.8 10.4 %collective-permute-start.10 = (f32[2,256,64]{2,1,0:T(8,128)S(1)}, f32[2,256,64]{2,1,0:T(8,128)S(1)}, u32[]{:S(2)}, u32[]{:S(2)}) collective-permute-start(f32[2,256,64]{2,1,0:T(8,128)S(1)} %get-tuple-element.348), channel_id=1, source_target_pairs={{0,1},{1,2},{2,3},{3,4},{4,5},{5,6},{6,7},{7,8},{8,9},{9,10},{10,1... | collective-permute-start | bytes 393224 | tf_op jit(solution)/shard_map/ppermute | solution.py:18
  370.3 9.3 %collective-permute-start.11 = (f32[2,256,64]{2,1,0:T(8,128)S(1)}, f32[2,256,64]{2,1,0:T(8,128)S(1)}, u32[]{:S(2)}, u32[]{:S(2)}) collective-permute-start(f32[2,256,64]{2,1,0:T(8,128)S(1)} %get-tuple-element.349), channel_id=1, source_target_pairs={{1,0},{2,1},{3,2},{4,3},{5,4},{6,5},{7,6},{8,7},{9,8},{10,9},{11,1... | collective-permute-start | bytes 393224 | tf_op jit(solution)/shard_map/ppermute | solution.py:21
  397.0 1.2 copy-start.6
  438.5 249.9 %collective-permute-start.12 = (f32[3,64,256]{2,1,0:T(8,128)S(1)}, f32[3,64,256]{2,1,0:T(8,128)S(1)}, u32[]{:S(2)}, u32[]{:S(2)}) collective-permute-start(f32[3,64,256]{2,1,0:T(8,128)S(1)} %get-tuple-element.335), channel_id=1, source_target_pairs={{0,16},{16,32},{32,48},{48,64},{64,80},{80,96},{96,112},{112,128},... | collective-permute-start | bytes 589832 | tf_op jit(solution)/shard_map/ppermute | solution.py:29
  443.9 244.5 %collective-permute-start.13 = (f32[3,64,256]{2,1,0:T(8,128)S(1)}, f32[3,64,256]{2,1,0:T(8,128)S(1)}, u32[]{:S(2)}, u32[]{:S(2)}) collective-permute-start(f32[3,64,256]{2,1,0:T(8,128)S(1)} %get-tuple-element.334), channel_id=1, source_target_pairs={{16,0},{32,16},{48,32},{64,48},{80,64},{96,80},{112,96},{128,112},... | collective-permute-start | bytes 589832 | tf_op jit(solution)/shard_map/ppermute | solution.py:29
  688.5 3.4 copy-start.10
  688.6 10.9 %collective-permute-start.14 = (f32[3,128,64]{2,1,0:T(8,128)S(1)}, f32[3,128,64]{2,1,0:T(8,128)S(1)}, u32[]{:S(2)}, u32[]{:S(2)}) collective-permute-start(f32[3,128,64]{2,1,0:T(8,128)S(1)} %get-tuple-element.343), channel_id=1, source_target_pairs={{0,1},{1,2},{2,3},{3,4},{4,5},{5,6},{6,7},{7,8},{8,9},{9,10},{10,1... | collective-permute-start | bytes 294920 | tf_op jit(solution)/shard_map/ppermute | solution.py:29
  692.8 8.9 %collective-permute-start.15 = (f32[3,128,64]{2,1,0:T(8,128)S(1)}, f32[3,128,64]{2,1,0:T(8,128)S(1)}, u32[]{:S(2)}, u32[]{:S(2)}) collective-permute-start(f32[3,128,64]{2,1,0:T(8,128)S(1)} %get-tuple-element.342), channel_id=1, source_target_pairs={{1,0},{2,1},{3,2},{4,3},{5,4},{6,5},{7,6},{8,7},{9,8},{10,9},{11,1... | collective-permute-start | bytes 294920 | tf_op jit(solution)/shard_map/ppermute | solution.py:29
Sparse Core Ops, SparseCore 0:
  98.6 250.3 all-reduce.6
  438.6 248.9 all-reduce.4
where the time goes:
time: 721 us; the launch traced here: 711 us
  waiting for transfers between devices  514 us (71%)
  local copies, waits for them, and re-layouts  53.5 us (7%)
  starting transfers between devices  50.7 us (7%)
  matrix products  37.1 us (5%)
  loops' own time  30.8 us (4%)
  between operations  15.7 us (2%)
  other arithmetic  9.27 us (1%)
    psum x2, waiting for transfers between devices, probe_update(): total_numer, total_denom = lax.psum((flat_numer, flat_denom), ('sy', 'sx'))  489 us
    another operation x2, loops' own time, local_terms(): lax.fori_loop(0, positions, place_patch, jnp.zeros((3,) + canvas.shape[1:...  30.4 us
    ppermute x8, starting transfers between devices, shifted(): lax.ppermute(value, axis, [(source, source + steps) for source in range(f...  26.3 us
    dynamic_update_slice x8, local copies, waits for them, and re-layouts, place_patch(): lax.dynamic_update_slice(running, existing + terms[number], (jnp.int32(0)...  22.4 us
    dot_general x16, matrix products, apply_right(): return jnp.einsum('bxy,yv->bxv', values, matrix, precision=HIGHEST)  19 us
    dot_general x16, matrix products, apply_left(): return jnp.einsum('ux,bxy->buy', matrix, values, precision=HIGHEST)  18.1 us
    gather x24, local copies, waits for them, and re-layouts  16.1 us
    ppermute x4, starting transfers between devices, extended(): lax.ppermute(lax.slice_in_dim(block, 0, width, axis=dim), axis, backward)  14.7 us
  transfers between devices with their start and end apart: 18, of which 11 were waited for; matrix products, arithmetic and copies ran while one was open for 1% of the time, Pallas kernels for 0%

commit v1 on v0

--- a/solution.py
+++ b/solution.py
@@ -121,7 +121,10 @@
     flat_numer = numerator.reshape(-1, extent * extent)
     flat_denom = denominator.reshape(extent * extent)
     flat_probe = probe_modes.reshape(-1, extent * extent)
-    total_numer, total_denom = lax.psum((flat_numer, flat_denom), ("sy", "sx"))
+    follow_rails = lambda x_local: jax.lax.psum(
+        jax.lax.psum(x_local, axis_name="sy"), axis_name="sx"
+    )
+    total_numer, total_denom = follow_rails((flat_numer, flat_denom))
     updated = flat_probe - PROBE_STEP * total_numer / (total_denom[None] + REGULAR)
     return updated.reshape(probe_modes.shape)
 

time: 721 us -> 767 us (1.064)
  waiting for transfers between devices: 514 us -> 551 us
  starting transfers between devices: 50.7 us -> 58.4 us
    psum x2 -> x4, waiting for transfers between devices: 489 us -> 533 us  [the longest x2 272 us: probe_update(): jax.lax.psum(x_local, axis_name='sy')]
  transfers between devices with their start and end apart: 18 -> 20, of which waited for: 11 -> 14; matrix products, arithmetic and copies ran while one was open for 1% -> 2% of each run, Pallas kernels for 0% -> 0%
where the time goes in v1:
time: 767 us; the launch traced here: 756 us
  waiting for transfers between devices  551 us (72%)
  starting transfers between devices  58.4 us (8%)
  local copies, waits for them, and re-layouts  51.9 us (7%)
  matrix products  38.3 us (5%)
  loops' own time  31.1 us (4%)
  between operations  15.1 us (2%)
  other arithmetic  9.31 us (1%)
    psum x2, waiting for transfers between devices, probe_update(): jax.lax.psum(x_local, axis_name='sy')  272 us
    psum x2, waiting for transfers between devices, probe_update(): jax.lax.psum(jax.lax.psum(x_local, axis_name='sy'), axis_name='sx')  261 us
    another operation x2, loops' own time, local_terms(): lax.fori_loop(0, positions, place_patch, jnp.zeros((3,) + canvas.shape[1:...  30.7 us
    ppermute x8, starting transfers between devices, shifted(): lax.ppermute(value, axis, [(source, source + steps) for source in range(f...  28 us
    dynamic_update_slice x8, local copies, waits for them, and re-layouts, place_patch(): lax.dynamic_update_slice(running, existing + terms[number], (jnp.int32(0)...  22.4 us
    dot_general x16, matrix products, apply_right(): return jnp.einsum('bxy,yv->bxv', values, matrix, precision=HIGHEST)  19.9 us
    dot_general x16, matrix products, apply_left(): return jnp.einsum('ux,bxy->buy', matrix, values, precision=HIGHEST)  18.4 us
    ppermute x4, starting transfers between devices, extended(): lax.ppermute(lax.slice_in_dim(block, block.shape[dim] - width, None, axis...  16.1 us
  transfers between devices with their start and end apart: 20, of which 14 were waited for; matrix products, arithmetic and copies ran while one was open for 2% of the time, Pallas kernels for 0%

profile of v1, /device:TPU:8, one launch (start us, length us, event | category | flops | bytes accessed | tf_op | source)
XLA Modules:
  0.0 755.6 jit_solution(8374984833916894047)
XLA Ops:
  8.1 1.9 collective-permute-start
  11.5 3.7 collective-permute-done.1
  15.4 3.8 collective-permute-start.2
  19.2 6.6 collective-permute-start.3
  25.9 2.4 collective-permute-done.2
  30.1 8.3 %while.38 = (s32[]{:T(128)}, f32[2,256,256]{2,1,0:T(8,128)S(1)}, s32[4,3]{1,0:T(4,128)S(1)}, f32[4,2,128,128]{3,2,1,0:T(8,128)S(1)}, s32[]{:T(128)}) while((s32[]{:T(128)}, f32[2,256,256]{2,1,0:T(8,128)S(1)}, s32[4,3]{1,0:T(4,128)S(1)}, f32[4,2,128,128]{3,2,1,0:T(8,128)S(1)}, s32[]{:T(128)}) %tuple.147), condition=%wide.while_cond.8, body=%wide.while_body.8.sunk | while | flops 2 | bytes 262261 | solution.py:61
  56.0 2.0 add_reduce_fusion.3
  58.2 29.6 %while.36 = (s32[]{:T(128)}, f32[3,256,256]{2,1,0:T(8,128)S(1)}, s32[4,2]{0,1:T(2,128)S(1)}, f32[4,3,128,128]{3,2,1,0:T(8,128)S(1)}, s32[]{:T(128)}, /*index=5*/s32[]{:T(128)}, s32[]{:T(128)}) while((s32[]{:T(128)}, f32[3,256,256]{2,1,0:T(8,128)S(1)}, s32[4,2]{0,1:T(2,128)S(1)}, f32[4,3,128,128]{3,2,1,0:T(8,128)S(1)}, s32[]{:T(128)}, ...), condition=%wide.region_5.6_spmd, body=%wide.region_4.5_spmd.sunk | while | flops 49160 | bytes 983237 | solution.py:113
  62.8 2.9 dynamic_update_slice.16
  70.3 2.8 dynamic_update_slice.16
  77.6 2.8 dynamic_update_slice.16
  85.1 2.8 dynamic_update_slice.16
  87.9 5.8 collective-permute-start.4
  97.2 2.7 collective-permute-start.6
  100.7 7.5 collective-permute-start.7
  112.6 6.7 collective-permute-start.8
  122.7 3.7 collective-permute-start.10
  126.4 4.9 collective-permute-start.11
  131.3 135.8 %all-reduce.15.cloned.1.call-done = (f32[4,16384]{1,0:T(4,128)}, f32[16384]{0:T(1024)}) async-done(((f32[4,16384]{1,0:T(4,128)}, f32[16384]{0:T(1024)}), (f32[4,16384]{1,0:T(4,128)}, f32[16384]{0:T(1024)})) %all-reduce.15.cloned.1.call-update) | async-done | bytes 327696 | tf_op jit(solution)/shard_map/psum | solution.py:125
  267.5 8.3 %while.39 = (s32[]{:T(128)}, f32[2,256,256]{2,1,0:T(8,128)S(1)}, s32[4,3]{1,0:T(4,128)S(1)}, f32[4,2,128,128]{3,2,1,0:T(8,128)S(1)}, s32[]{:T(128)}) while((s32[]{:T(128)}, f32[2,256,256]{2,1,0:T(8,128)S(1)}, s32[4,3]{1,0:T(4,128)S(1)}, f32[4,2,128,128]{3,2,1,0:T(8,128)S(1)}, s32[]{:T(128)}) %tuple.173), condition=%wide.while_cond.9, body=%wide.while_body.9.sunk | while | flops 2 | bytes 262261 | solution.py:61
  275.9 126.7 %all-reduce.11.cloned.1.call-done = (f32[4,16384]{1,0:T(4,128)}, f32[16384]{0:T(1024)}) async-done(((f32[4,16384]{1,0:T(4,128)}, f32[16384]{0:T(1024)}), (f32[4,16384]{1,0:T(4,128)}, f32[16384]{0:T(1024)})) %all-reduce.11.cloned.1.call-update) | async-done | bytes 327696 | tf_op jit(solution)/shard_map/psum | solution.py:124
  422.9 2.0 add_reduce_fusion.1
  425.0 29.5 %while.37 = (s32[]{:T(128)}, f32[3,256,256]{2,1,0:T(8,128)S(1)}, s32[4,2]{0,1:T(2,128)S(1)}, f32[4,3,128,128]{3,2,1,0:T(8,128)S(1)}, s32[]{:T(128)}, /*index=5*/s32[]{:T(128)}, s32[]{:T(128)}) while((s32[]{:T(128)}, f32[3,256,256]{2,1,0:T(8,128)S(1)}, s32[4,2]{0,1:T(2,128)S(1)}, f32[4,3,128,128]{3,2,1,0:T(8,128)S(1)}, s32[]{:T(128)}, ...), condition=%wide.region_18.19_spmd, body=%wide.region_17.18_spmd.sunk | while | flops 49160 | bytes 983237 | solution.py:113
  429.6 2.9 dynamic_update_slice.17
  437.0 2.8 dynamic_update_slice.17
  444.3 2.8 dynamic_update_slice.17
  451.7 2.8 dynamic_update_slice.17
  458.2 3.0 collective-permute-done.13
  461.4 3.2 collective-permute-start.14
  465.7 4.8 collective-permute-start.15
  474.8 136.0 %all-reduce.13.cloned.1.call-done = (f32[4,16384]{1,0:T(4,128)}, f32[16384]{0:T(1024)}) async-done(((f32[4,16384]{1,0:T(4,128)}, f32[16384]{0:T(1024)}), (f32[4,16384]{1,0:T(4,128)}, f32[16384]{0:T(1024)})) %all-reduce.13.cloned.1.call-update) | async-done | bytes 327696 | tf_op jit(solution)/shard_map/psum | solution.py:125
  611.5 134.6 %all-reduce.9.cloned.1.call-done = (f32[4,16384]{1,0:T(4,128)}, f32[16384]{0:T(1024)}) async-done(((f32[4,16384]{1,0:T(4,128)}, f32[16384]{0:T(1024)}), (f32[4,16384]{1,0:T(4,128)}, f32[16384]{0:T(1024)})) %all-reduce.9.cloned.1.call-update) | async-done | bytes 327696 | tf_op jit(solution)/shard_map/psum | solution.py:124
  (205 shorter events, 89.3 us)
Async XLA Ops:
  7.2 259.9 %all-reduce.15.cloned.1.call-start = ((), (), s32[]{:S(2)}) async-start(), calls=%async_computation.3 | async-start | bytes 655360 | tf_op jit(solution)/shard_map/psum | solution.py:125
  7.2 4.1 copy-start.13
  8.1 3.4 copy-start.8
  8.1 3.3 collective-permute-start
  10.0 5.2 collective-permute-start.1
  15.2 10.6 %copy-start.11 = (f32[2,2,128,128]{3,2,1,0:T(8,128)S(1)}, f32[2,2,128,128]{3,2,1,0:T(8,128)}, u32[]{:S(2)}) copy-start(f32[2,2,128,128]{3,2,1,0:T(8,128)} %param.25) | copy-start | bytes 786436
  15.4 12.9 %collective-permute-start.2 = (f32[2,256,64]{2,1,0:T(8,128)S(1)}, f32[2,256,64]{2,1,0:T(8,128)S(1)}, u32[]{:S(2)}, u32[]{:S(2)}) collective-permute-start(f32[2,256,64]{2,1,0:T(8,128)S(1)} %get-tuple-element.358), channel_id=1, source_target_pairs={{0,1},{1,2},{2,3},{3,4},{4,5},{5,6},{6,7},{7,8},{8,9},{9,10},{10,1... | collective-permute-start | bytes 393224 | tf_op jit(solution)/shard_map/ppermute | solution.py:18
  19.2 10.5 %collective-permute-start.3 = (f32[2,256,64]{2,1,0:T(8,128)S(1)}, f32[2,256,64]{2,1,0:T(8,128)S(1)}, u32[]{:S(2)}, u32[]{:S(2)}) collective-permute-start(f32[2,256,64]{2,1,0:T(8,128)S(1)} %get-tuple-element.359), channel_id=1, source_target_pairs={{1,0},{2,1},{3,2},{4,3},{5,4},{6,5},{7,6},{8,7},{9,8},{10,9},{11,1... | collective-permute-start | bytes 393224 | tf_op jit(solution)/shard_map/ppermute | solution.py:21
  46.4 1.2 copy-start.9
  87.9 7.2 copy-start.7
  87.9 7.4 collective-permute-start.4
  93.7 3.3 collective-permute-start.5
  97.2 11.9 %collective-permute-start.6 = (f32[3,128,64]{2,1,0:T(8,128)S(1)}, f32[3,128,64]{2,1,0:T(8,128)S(1)}, u32[]{:S(2)}, u32[]{:S(2)}) collective-permute-start(f32[3,128,64]{2,1,0:T(8,128)S(1)} %get-tuple-element.349), channel_id=1, source_target_pairs={{0,1},{1,2},{2,3},{3,4},{4,5},{5,6},{6,7},{7,8},{8,9},{9,10},{10,1... | collective-permute-start | bytes 294920 | tf_op jit(solution)/shard_map/ppermute | solution.py:29
  100.7 10.7 %collective-permute-start.7 = (f32[3,128,64]{2,1,0:T(8,128)S(1)}, f32[3,128,64]{2,1,0:T(8,128)S(1)}, u32[]{:S(2)}, u32[]{:S(2)}) collective-permute-start(f32[3,128,64]{2,1,0:T(8,128)S(1)} %get-tuple-element.348), channel_id=1, source_target_pairs={{1,0},{2,1},{3,2},{4,3},{5,4},{6,5},{7,6},{8,7},{9,8},{10,9},{11,1... | collective-permute-start | bytes 294920 | tf_op jit(solution)/shard_map/ppermute | solution.py:29
  112.6 9.0 %collective-permute-start.8 = (f32[2,64,128]{2,1,0:T(8,128)S(1)}, f32[2,64,128]{2,1,0:T(8,128)S(1)}, u32[]{:S(2)}, u32[]{:S(2)}) collective-permute-start(f32[2,64,128]{2,1,0:T(8,128)S(1)} %get-tuple-element.363), channel_id=1, source_target_pairs={{0,16},{16,32},{32,48},{48,64},{64,80},{80,96},{96,112},{112,128},... | collective-permute-start | bytes 196616 | tf_op jit(solution)/shard_map/ppermute | solution.py:18
  119.4 3.1 collective-permute-start.9
  121.6 281.0 %all-reduce.11.cloned.1.call-start = ((), (), s32[]{:S(2)}) async-start(), calls=%async_computation.1 | async-start | bytes 655360 | tf_op jit(solution)/shard_map/psum | solution.py:124
  122.7 144.5 %collective-permute-start.10 = (f32[2,256,64]{2,1,0:T(8,128)S(1)}, f32[2,256,64]{2,1,0:T(8,128)S(1)}, u32[]{:S(2)}, u32[]{:S(2)}) collective-permute-start(f32[2,256,64]{2,1,0:T(8,128)S(1)} %get-tuple-element.352), channel_id=1, source_target_pairs={{0,1},{1,2},{2,3},{3,4},{4,5},{5,6},{6,7},{7,8},{8,9},{9,10},{10,1... | collective-permute-start | bytes 393224 | tf_op jit(solution)/shard_map/ppermute | solution.py:18
  126.4 140.8 %collective-permute-start.11 = (f32[2,256,64]{2,1,0:T(8,128)S(1)}, f32[2,256,64]{2,1,0:T(8,128)S(1)}, u32[]{:S(2)}, u32[]{:S(2)}) collective-permute-start(f32[2,256,64]{2,1,0:T(8,128)S(1)} %get-tuple-element.353), channel_id=1, source_target_pairs={{1,0},{2,1},{3,2},{4,3},{5,4},{6,5},{7,6},{8,7},{9,8},{10,9},{11,1... | collective-permute-start | bytes 393224 | tf_op jit(solution)/shard_map/ppermute | solution.py:21
  267.1 343.7 %all-reduce.13.cloned.1.call-start = ((), (), s32[]{:S(2)}) async-start(), calls=%async_computation.2 | async-start | bytes 655360 | tf_op jit(solution)/shard_map/psum | solution.py:125
  275.8 129.5 %copy-start = (f32[4,128,128]{2,1,0:T(8,128)}, f32[4,128,128]{2,1,0:T(8,128)S(1)}, u32[]{:S(2)}) copy-start(f32[4,128,128]{2,1,0:T(8,128)S(1)} %slice_bitcast_fusion) | copy-start | bytes 786436
  275.8 127.6 %copy-start.12 = (f32[2,2,128,128]{3,2,1,0:T(8,128)S(1)}, f32[2,2,128,128]{3,2,1,0:T(8,128)}, u32[]{:S(2)}) copy-start(f32[2,2,128,128]{3,2,1,0:T(8,128)} %param.25) | copy-start | bytes 786436
  275.9 129.5 %copy-start.2 = (f32[4,128,128]{2,1,0:T(8,128)}, f32[4,128,128]{2,1,0:T(8,128)S(1)}, u32[]{:S(2)}) copy-start(f32[4,128,128]{2,1,0:T(8,128)S(1)} %slice_bitcast_fusion.2) | copy-start | bytes 786436
  454.5 3.7 collective-permute-start.12
  455.8 2.1 copy-start.6
  456.5 1.5 copy-start.1
  456.5 1.5 copy-start.3
  456.5 4.7 collective-permute-start.13
  461.4 10.5 %collective-permute-start.14 = (f32[3,128,64]{2,1,0:T(8,128)S(1)}, f32[3,128,64]{2,1,0:T(8,128)S(1)}, u32[]{:S(2)}, u32[]{:S(2)}) collective-permute-start(f32[3,128,64]{2,1,0:T(8,128)S(1)} %get-tuple-element.347), channel_id=1, source_target_pairs={{0,1},{1,2},{2,3},{3,4},{4,5},{5,6},{6,7},{7,8},{8,9},{9,10},{10,1... | collective-permute-start | bytes 294920 | tf_op jit(solution)/shard_map/ppermute | solution.py:29
  465.5 280.6 %all-reduce.9.cloned.1.call-start = ((), (), s32[]{:S(2)}) async-start(), calls=%async_computation | async-start | bytes 655360 | tf_op jit(solution)/shard_map/psum | solution.py:124
  465.7 7.9 %collective-permute-start.15 = (f32[3,128,64]{2,1,0:T(8,128)S(1)}, f32[3,128,64]{2,1,0:T(8,128)S(1)}, u32[]{:S(2)}, u32[]{:S(2)}) collective-permute-start(f32[3,128,64]{2,1,0:T(8,128)S(1)} %get-tuple-element.346), channel_id=1, source_target_pairs={{1,0},{2,1},{3,2},{4,3},{5,4},{6,5},{7,6},{8,7},{9,8},{10,9},{11,1... | collective-permute-start | bytes 294920 | tf_op jit(solution)/shard_map/ppermute | solution.py:29
  610.8 136.1 %copy-start.5 = (f32[4,16384]{1,0:T(4,128)S(1)}, f32[4,16384]{1,0:T(4,128)}, u32[]{:S(2)}) copy-start(f32[4,16384]{1,0:T(4,128)} %copy-done.4) | copy-start | bytes 786436
  (2 other events, 1.9 us)
Sparse Core Ops, SparseCore 0:
  121.7 145.3 all-reduce.14
  270.0 132.4 all-reduce.10
  465.6 145.1 all-reduce.12
  613.6 132.4 all-reduce.8
